TPU v7x, 512 devices: a whole 4x8x8 slice. The times are simulated.
512 devices in a mesh: slab: 128 (over y, z, core), case: 4 (over x).
Axes of the slice: x: 4, y: 8, z: 8, core: 2. Of those that a mesh axis runs over, the one named last changes fastest.
Arguments:
- pressure: float32 [64, 512], replicated, may hold values from -9 to 9
- panel: int32 [1536, 4, 128], P('slab'), may hold values from 0 to 511
- flags: int32 [1536, 4, 128], P('slab'), may hold values 0 or 1
- diagonal: float32 [1536, 4, 128], P('slab'), may hold values from 0.25 to 4
Outputs:
- fields: float32 [64, 1536, 4, 128], P('case', 'slab')
- gram: float32 [64, 64], P('case')
- cross: float32 [64, 64], P('case')
All inputs are finite; a program needn't handle non-finite values. No bound on the sum of `flags` on one device may be relied on, other than what follows from the above.
Results may differ from a plain program's by a relative error of at most 0.00005.
Values sent between devices are 32-bit elements; how exact they have to be, the bound alone decides.
A program may use at most 64 MiB of HBM per device.

v0:
```python
import jax
import jax.numpy as jnp
from jax import lax
from jax.sharding import PartitionSpec as P

damping = 0.7
penalty = 4.0
highest = lax.Precision.HIGHEST


def with_halo(cells, sides, width):
    for axis, dim in sides:
        count = lax.axis_size(axis)
        ends = count - 1
        head = lax.slice_in_dim(cells, 0, width, axis=dim)
        tail = lax.slice_in_dim(cells, cells.shape[dim] - width, cells.shape[dim], axis=dim)
        cells = jnp.concatenate(
            [
                lax.ppermute(tail, axis, [(i, (i + 1) % count) for i in range(ends)]),
                cells,
                lax.ppermute(head, axis, [((i + 1) % count, i) for i in range(ends)]),
            ],
            axis=dim,
        )
    return cells


def from_behind(x, axis, by):
    count = lax.axis_size(axis)
    pairs = [(i, i + by) for i in range(count) if 0 <= i + by < count]
    return lax.ppermute(x, axis, pairs)


def transverse(field):
    beside_all = jnp.roll(field, 1, axis=-1) + jnp.roll(field, -1, axis=-1)
    zero_row = jnp.zeros_like(field[..., :1, :])
    inward = jnp.concatenate([zero_row, field[..., :-1, :]], axis=-2)
    outward = jnp.concatenate([field[..., 1:, :], zero_row], axis=-2)
    return beside_all + inward + outward


def stencil(field, below, above, coeff, weight):
    return (coeff + 2.0 * weight + 4.0) * field - weight * (below + above) - transverse(field)


def apply_halo(field, coeff, weight):
    padded = with_halo(field, (("slab", 1),), 1)
    return stencil(field, padded[:, :-2], padded[:, 2:], coeff, weight)


def smooth_halo(field, rhs, coeff, weight):
    return field + damping * (rhs - apply_halo(field, coeff, weight)) / (coeff + 2.0 * weight + 4.0)


def restrict(fine):
    even = fine[:, 0::2]
    odd = fine[:, 1::2]
    lower = from_behind(fine[:, -1:], "slab", 1)
    odd_before = jnp.concatenate([lower, odd[:, :-1]], axis=1)
    return 0.5 * even + 0.25 * (odd + odd_before)


def prolong(coarse):
    upper = from_behind(coarse[:, :1], "slab", -1)
    following = jnp.concatenate([coarse[:, 1:], upper], axis=1)
    middle = 0.5 * (coarse + following)
    stacked = jnp.stack([coarse, middle], axis=2)
    shape = coarse.shape
    return stacked.reshape(shape[0], 2 * shape[1], shape[2], shape[3])


def coarsest(rhs, coeff, weight):
    field = damping * rhs / (coeff + 2.0 * weight + 4.0)
    for sweep in range(3):
        field = smooth_halo(field, rhs, coeff, weight)
    return field


def vcycle(rhs, coeff, level):
    weight = 0.25**level
    if level == 2:
        return coarsest(rhs, coeff, weight)
    field = damping * rhs / (coeff + 2.0 * weight + 4.0)
    field = smooth_halo(field, rhs, coeff, weight)
    leftover = rhs - apply_halo(field, coeff, weight)
    coarse_coeff = 0.5 * (coeff[0::2] + coeff[1::2])
    field = field + prolong(vcycle(restrict(leftover), coarse_coeff, level + 1))
    for sweep in range(2):
        field = smooth_halo(field, rhs, coeff, weight)
    return field


def local(pressure, panel, flags, diagonal):
    layers, radial, beside_all = panel.shape
    slabs = lax.axis_size("slab")
    groups = lax.axis_size("case")
    per_group = pressure.shape[0] // groups
    total_layers = layers * slabs
    own_group = lax.axis_index("case")
    case_rows = lax.dynamic_slice_in_dim(pressure, own_group * per_group, per_group, 0)
    coeff = diagonal + penalty * flags.astype(jnp.float32)
    keep = 1.0 - flags.astype(jnp.float32)
    positions = (lax.axis_index("slab") * layers + jnp.arange(layers)).astype(jnp.float32)
    span = (1.0 + 2.0 * positions / total_layers)[:, None, None]
    loads = jnp.take(case_rows, panel, axis=1) * span * keep
    fields = vcycle(loads, coeff, 0)
    images = apply_halo(fields, coeff, 1.0)
    scale = 1.0 / (total_layers * radial * beside_all)
    contract = (((1,), (1,)), ((), ()))
    images_flat = images.reshape(per_group, -1)
    loads_flat = loads.reshape(per_group, -1)
    piece = lax.all_gather(fields, "case", axis=0, tiled=True)
    piece_flat = piece.reshape(piece.shape[0], -1)
    gram_block = lax.dot_general(
        images_flat, piece_flat, contract, precision=highest, preferred_element_type=jnp.float32
    )
    cross_block = lax.dot_general(
        loads_flat, piece_flat, contract, precision=highest, preferred_element_type=jnp.float32
    )
    gram_rows, cross_rows = lax.psum((gram_block, cross_block), "slab")
    return (fields, gram_rows * scale, cross_rows * scale)


def solution(mesh):
    in_specs = (P(), P("slab", None, None), P("slab", None, None), P("slab", None, None))
    out_specs = (P("case", "slab", None, None), P("case", None), P("case", None))
    return jax.shard_map(local, mesh=mesh, in_specs=in_specs, out_specs=out_specs, check_vma=False)
```

profile of v0, /device:TPU:1, one launch (start us, length us, event | category | flops | bytes accessed | tf_op | source)
XLA Modules:
  0.0 727.0 jit_solution(7467663255318855311)
XLA Ops:
  8.9 20.9 %gather_fusion = f32[6144,16]{1,0:T(8,128)} fusion(f32[16,512]{0,1:T(8,128)S(1)} %copy.21, s32[6144]{0:T(1024)S(1)} %broadcast_clamp_fusion), kind=kCustom, calls=%fused_computation | custom fusion | bytes 811008 | tf_op jit(solution)/shard_map/jit(_take)/gather | solution.py:105
  29.9 2.3 copy.13
  32.4 5.4 collective-permute-start
  37.8 4.7 collective-permute-start.1
  46.1 2.4 collective-permute-start.3
  48.6 3.2 collective-permute-done.3
  55.7 4.1 collective-permute-start.5
  61.7 3.3 collective-permute-done.6
  65.4 4.2 collective-permute-start.7
  71.5 4.2 collective-permute-done.8
  79.2 4.5 collective-permute-start.10
  83.8 1.9 collective-permute-start.11
  85.7 3.3 collective-permute-done.11
  89.3 4.2 collective-permute-start.12
  95.5 4.2 collective-permute-done.13
  101.9 2.4 collective-permute-start.15
  104.4 4.0 collective-permute-done.15
  110.5 3.3 collective-permute-done.16
  114.1 4.2 collective-permute-start.17
  120.3 4.2 collective-permute-done.18
  126.8 2.4 collective-permute-start.20
  129.3 4.0 collective-permute-done.20
  135.4 3.3 collective-permute-done.21
  139.2 3.4 collective-permute-start.22
  144.7 4.1 collective-permute-done.23
  151.6 2.4 collective-permute-start.25
  154.1 4.0 collective-permute-done.25
  159.3 1.9 copy.16
  164.0 2.4 collective-permute-start.27
  166.8 56.8 %all-gather.2.cloned.1.call-done = f32[64,12,4,128]{3,0,2,1:T(8,128)} async-done(((f32[16,12,4,128]{3,0,2,1:T(8,128)}), f32[64,12,4,128]{3,0,2,1:T(8,128)}) %all-gather.2.cloned.1.call-update) | async-done | bytes 1572880 | tf_op jit(solution)/shard_map/all_gather | solution.py:112
  223.6 2.9 convolution_bitcast_fusion
  228.0 491.5 %all-reduce.24 = (f32[16,64]{1,0:T(8,128)S(1)}, f32[16,64]{1,0:T(8,128)S(1)}) all-reduce(f32[16,64]{1,0:T(8,128)S(1)} %convolution_bitcast_fusion.1, f32[16,64]{1,0:T(8,128)S(1)} %convolution_bitcast_fusion), channel_id=1, replica_groups=mesh['slab'=128,'case'=4] {'slab'}, use_global_device_ids=true, to_apply=%region_0.1 | all-reduce | flops 2048 | bytes 16384 | tf_op jit(solution)/shard_map/psum | solution.py:120
  (133 shorter events, 42.1 us)
Async XLA Ops:
  7.2 216.5 %all-gather.2.cloned.1.call-start = ((), (), s32[]{:S(2)}) async-start(), calls=%async_computation | async-start | bytes 1966080 | tf_op jit(solution)/shard_map/all_gather | solution.py:112
  29.9 2.4 copy-start.4
  32.4 10.5 %collective-permute-start = (f32[16,1,4,128]{3,0,2,1:T(8,128)S(1)}, f32[16,1,4,128]{3,0,2,1:T(8,128)S(1)}, u32[]{:S(2)}, u32[]{:S(2)}) collective-permute-start(f32[16,1,4,128]{3,0,2,1:T(8,128)S(1)} %get-tuple-element.57), channel_id=1, source_target_pairs={{0,4},{4,8},{8,12},{12,16},{16,20},{20,24},{24,28},{28,32},{32,36}... | collective-permute-start | bytes 98312 | tf_op jit(solution)/shard_map/ppermute | solution.py:19
  37.8 5.5 collective-permute-start.1
  44.2 4.4 collective-permute-start.2
  46.1 5.7 collective-permute-start.3
  52.2 3.1 collective-permute-start.4
  55.7 6.0 collective-permute-start.5
  59.7 5.2 collective-permute-start.6
  65.4 6.2 collective-permute-start.7
  69.6 6.1 collective-permute-start.8
  75.9 3.1 collective-permute-start.9
  79.2 6.5 collective-permute-start.10
  83.8 5.2 collective-permute-start.11
  89.3 6.2 collective-permute-start.12
  93.5 6.1 collective-permute-start.13
  100.0 4.4 collective-permute-start.14
  101.9 6.4 collective-permute-start.15
  108.5 5.2 collective-permute-start.16
  114.1 6.2 collective-permute-start.17
  118.3 6.1 collective-permute-start.18
  124.9 4.4 collective-permute-start.19
  126.8 6.4 collective-permute-start.20
  133.4 5.2 collective-permute-start.21
  139.2 5.4 collective-permute-start.22
  142.7 6.1 collective-permute-start.23
  149.7 4.4 collective-permute-start.24
  151.6 6.4 collective-permute-start.25
  159.3 7.1 copy-start.1
  162.0 64.5 %collective-permute-start.26 = (f32[16,1,4,128]{3,0,2,1:T(8,128)S(1)}, f32[16,1,4,128]{3,0,2,1:T(8,128)S(1)}, u32[]{:S(2)}, u32[]{:S(2)}) collective-permute-start(f32[16,1,4,128]{3,0,2,1:T(8,128)S(1)} %get-tuple-element.25), channel_id=1, source_target_pairs={{0,4},{4,8},{8,12},{12,16},{16,20},{20,24},{24,28},{28,32},{32,36}... | collective-permute-start | bytes 98312 | tf_op jit(solution)/shard_map/ppermute | solution.py:19
  164.0 62.6 %collective-permute-start.27 = (f32[16,1,4,128]{3,0,2,1:T(8,128)S(1)}, f32[16,1,4,128]{3,0,2,1:T(8,128)S(1)}, u32[]{:S(2)}, u32[]{:S(2)}) collective-permute-start(f32[16,1,4,128]{3,0,2,1:T(8,128)S(1)} %get-tuple-element.26), channel_id=1, source_target_pairs={{4,0},{8,4},{12,8},{16,12},{20,16},{24,20},{28,24},{32,28},{36,32}... | collective-permute-start | bytes 98312 | tf_op jit(solution)/shard_map/ppermute | solution.py:21
  223.6 2.9 copy-start.2
  (2 other events, 4.0 us)
Sparse Core Ops, SparseCore 0:
  159.4 64.1 all-gather.1
where the time goes:
time: 731 us; the launch traced here: 727 us
  blocking collectives  492 us (67%)
  waiting for transfers between devices  104 us (14%)
  starting transfers between devices  75.5 us (10%)
  local copies, waits for them, and re-layouts  29.9 us (4%)
  between operations  14.9 us (2%)
    psum x1, blocking collectives, local(): gram_rows, cross_rows = lax.psum((gram_block, cross_block), 'slab')  492 us
    all_gather x1, waiting for transfers between devices, local(): piece = lax.all_gather(fields, 'case', axis=0, tiled=True)  56.8 us
    ppermute x12, starting transfers between devices, with_halo(): lax.ppermute(tail, axis, [(i, (i + 1) % count) for i in range(ends)])  39.6 us
    ppermute x12, waiting for transfers between devices, with_halo(): lax.ppermute(head, axis, [((i + 1) % count, i) for i in range(ends)])  38.7 us
    ppermute x12, starting transfers between devices, with_halo(): lax.ppermute(head, axis, [((i + 1) % count, i) for i in range(ends)])  28.2 us
    gather x2, local copies, waits for them, and re-layouts, local(): loads = jnp.take(case_rows, panel, axis=1) * span * keep  23.3 us
  transfers between devices with their start and end apart: 29, of which 16 were waited for; matrix products, arithmetic and copies ran while one was open for 1% of the time, Pallas kernels for 0%

commit v1 on v0

v1 whole, which is shorter than its diff:
```python
import functools

import jax
import jax.numpy as jnp
from jax import lax
from jax.experimental import pallas as pl
from jax.experimental.pallas import tpu as pltpu
from jax.sharding import PartitionSpec as P

MESH = pl.DeviceIdType.MESH
ZSIZE = 8
YSIZE = 8
CORES = 2
CASES = 4
REACH = 3
BASE = 29
highest = lax.Precision.HIGHEST


def halo_kernel(slabs, panel, flags, diagonal, panel_out, flags_out, diagonal_out, send, recv, own):
    slab = lax.axis_index("slab")
    barrier = pltpu.get_barrier_semaphore()
    shifts = [d for d in range(-REACH, REACH + 1) if d != 0]
    for d in shifts:
        there = lax.rem(slab + d + slabs, slabs)
        pl.semaphore_signal(barrier, inc=1, device_id={"slab": there}, device_id_type=MESH)
    locals_ = []
    for n, (src, dst) in enumerate(((panel, panel_out), (flags, flags_out), (diagonal, diagonal_out))):
        copy = pltpu.make_async_copy(src, dst.at[REACH], own.at[n])
        copy.start()
        locals_.append(copy)
    pl.semaphore_wait(barrier, len(shifts))
    copies = []
    layers = panel.shape[0]
    for d in sorted(shifts, key=lambda d: -abs(d)):
        there = lax.rem(slab + d + slabs, slabs)
        slot = REACH - d
        start, count = {3: (layers - 5, 5), -3: (0, 6)}.get(d, (0, layers))
        for n, (src, dst) in enumerate(((panel, panel_out), (flags, flags_out), (diagonal, diagonal_out))):
            copy = pltpu.make_async_remote_copy(
                src_ref=src.at[pl.ds(start, count)],
                dst_ref=dst.at[slot, pl.ds(start, count)],
                send_sem=send.at[n, slot],
                recv_sem=recv.at[n, slot],
                device_id={"slab": there},
                device_id_type=MESH,
            )
            copy.start()
            copies.append(copy)
    for copy in locals_:
        copy.wait()
    for copy in copies:
        copy.wait()


def exchange_halo(panel, flags, diagonal, slabs):
    shape = (2 * REACH + 1,) + panel.shape
    anyspace = pl.BlockSpec(memory_space=pl.ANY)
    return pl.pallas_call(
        functools.partial(halo_kernel, slabs),
        out_shape=[
            jax.ShapeDtypeStruct(shape, jnp.int32),
            jax.ShapeDtypeStruct(shape, jnp.int32),
            jax.ShapeDtypeStruct(shape, jnp.float32),
        ],
        in_specs=[anyspace] * 3,
        out_specs=[anyspace] * 3,
        scratch_shapes=[
            pltpu.SemaphoreType.DMA((3, 2 * REACH + 1)),
            pltpu.SemaphoreType.DMA((3, 2 * REACH + 1)),
            pltpu.SemaphoreType.DMA((3,)),
        ],
        compiler_params=pltpu.CompilerParams(collective_id=1, has_side_effects=True),
        name="halo",
    )(panel, flags, diagonal)


def lateral(v):
    flat = v.reshape(-1, v.shape[-1])
    sides = pltpu.roll(flat, 1, 1) + pltpu.roll(flat, flat.shape[1] - 1, 1)
    edge = jnp.zeros_like(v[:1])
    inward = jnp.concatenate([edge, v[:-1]], axis=0)
    outward = jnp.concatenate([v[1:], edge], axis=0)
    return sides.reshape(v.shape) + (inward + outward)


def spread(row):
    return jnp.broadcast_to(row[:, None, None, :], (row.shape[0], 1, 8, row.shape[1]))


def lookup(blocks, panel_row):
    out = []
    for r in range(panel_row.shape[0]):
        where = jnp.broadcast_to(panel_row[r : r + 1], (8, panel_row.shape[1]))
        low = where & 127
        high = where >> 7
        halves = []
        for pieces in blocks:
            found = jnp.take_along_axis(pieces[0], low, axis=1)
            for j in range(1, len(pieces)):
                found = jnp.where(high == j, jnp.take_along_axis(pieces[j], low, axis=1), found)
            halves.append(found)
        out.append(jnp.stack(halves))
    return jnp.stack(out)


def vcycle_kernel(total, pressure, panel, flags, diagonal, fields, ext, loads, chunk_diag,
                  b0, c0, v0a, v0b, r0, w0, d0, b1, c1, v1a, v1b, r1, w1, d1, b2, v2a, v2b, w2):
    slab = lax.axis_index("slab")
    group = lax.axis_index("case")
    own = fields.shape[1]
    pad = REACH * own
    cases = fields.shape[0]
    first = pl.multiple_of(group * cases, cases)
    blocks = [
        [pressure[pl.ds(first + 8 * h, 8), 128 * j : 128 * j + 128] for j in range(pressure.shape[1] // 128)]
        for h in range(cases // 8)
    ]

    def inside(p, level):
        g = p + slab * (own >> level)
        return (g >= pad >> level) & (g < (total + pad) >> level)

    def span_of(p):
        at = (p + slab * own - pad).astype(jnp.float32)
        return 1.0 + 2.0 * at / total

    def setup(i, _):
        p = i + (pad - BASE)
        held = flags[p].astype(jnp.float32)
        coeff = diagonal[p] + 4.0 * held
        c0[i] = coeff
        full = coeff + 6.0
        within = inside(p, 0)
        w = spread(jnp.where(within, 0.7 / full, 0.0))
        factor = spread(jnp.where(within, (1.0 - held) * span_of(p), 0.0))
        w0[i] = w
        d0[i] = spread(full)
        rhs = lookup(blocks, panel[p]) * factor
        b0[i] = rhs
        v0a[i] = w * rhs
        return 0

    lax.fori_loop(0, 71, setup, 0)

    def sweep(src, dst, rhs, w, weight, base, low, high):
        def body(i, _):
            v = src[i]
            near = src[i - 1] + src[i + 1]
            if weight != 1.0:
                near = weight * near
            dst[i] = 0.3 * v + w[i] * (rhs[i] + near + lateral(v))
            return 0

        lax.fori_loop(low + base, high + base, body, 0)

    def residual(src, dst, rhs, full, weight, base, low, high, level):
        def body(i, _):
            v = src[i]
            near = src[i - 1] + src[i + 1]
            if weight != 1.0:
                near = weight * near
            left = rhs[i] - full[i] * v + (near + lateral(v))
            dst[i] = jnp.where(inside(i + ((pad >> level) - base), level), left, 0.0)
            return 0

        lax.fori_loop(low + base, high + base, body, 0)

    def restrict(fine, fine_base, cfine, rhs, ccoarse, w, full, vinit, weight, base, low, high, level):
        def body(k, _):
            at = 2 * k + (fine_base + 2 * low)
            i = k + (low + base)
            value = 0.5 * fine[at] + 0.25 * (fine[at + 1] + fine[at - 1])
            coeff = 0.5 * (cfine[at] + cfine[at + 1])
            diag = coeff + (2.0 * weight + 4.0)
            if ccoarse is not None:
                ccoarse[i] = coeff
                full[i] = spread(diag)
            scale = spread(jnp.where(inside(k + (low + (pad >> level)), level), 0.7 / diag, 0.0))
            w[i] = scale
            rhs[i] = value
            vinit[i] = scale * value
            return 0

        lax.fori_loop(0, high - low, body, 0)

    def prolong(coarse, coarse_base, v, base, low, high, level):
        def body(k, _):
            here = coarse[k + (low + coarse_base)]
            after = coarse[k + (low + coarse_base + 1)]
            at = 2 * k + (2 * low + base)
            p = 2 * k + (2 * low + (pad >> level))
            v[at] = v[at] + jnp.where(inside(p, level), here, 0.0)
            v[at + 1] = v[at + 1] + jnp.where(inside(p + 1, level), 0.5 * (here + after), 0.0)
            return 0

        lax.fori_loop(0, high - low, body, 0)

    sweep(v0a, v0b, b0, w0, 1.0, BASE, -28, 41)
    residual(v0b, r0, b0, d0, 1.0, BASE, -27, 40, 0)
    restrict(r0, BASE, c0, b1, c1, w1, d1, v1a, 0.25, 14, -13, 20, 1)
    sweep(v1a, v1b, b1, w1, 0.25, 14, -12, 19)
    residual(v1b, r1, b1, d1, 0.25, 14, -11, 18, 1)
    restrict(r1, 14, c1, b2, None, w2, None, v2a, 0.0625, 6, -5, 9, 2)
    sweep(v2a, v2b, b2, w2, 0.0625, 6, -4, 8)
    sweep(v2b, v2a, b2, w2, 0.0625, 6, -3, 7)
    sweep(v2a, v2b, b2, w2, 0.0625, 6, -2, 6)
    prolong(v2b, 6, v1b, 14, -2, 5, 1)
    sweep(v1b, v1a, b1, w1, 0.25, 14, -3, 9)
    sweep(v1a, v1b, b1, w1, 0.25, 14, -2, 8)
    prolong(v1b, 14, v0b, BASE, -2, 7, 0)
    even = v1b[7 + 14]
    v0b[14 + BASE] = v0b[14 + BASE] + jnp.where(inside(14 + pad, 0), even, 0.0)
    sweep(v0b, v0a, b0, w0, 1.0, BASE, -2, 14)

    def last(k, _):
        i = k + (BASE - 1)
        v = v0a[i]
        near = v0a[i - 1] + v0a[i + 1]
        ext[k] = 0.3 * v + w0[i] * (b0[i] + near + lateral(v))
        return 0

    lax.fori_loop(0, own + 2, last, 0)
    for f in range(own):
        for r in range(fields.shape[2]):
            fields[:, f, r, :] = ext[f + 1, r].reshape(cases, 128)

    share = own // CASES
    for j in range(share):
        p = group * share + (pad + j)
        held = flags[p].astype(jnp.float32)
        factor = spread((1.0 - held) * span_of(p))
        chunk_diag[j] = spread(diagonal[p] + 4.0 * held + 6.0)
        every = [
            [pressure[8 * h : 8 * h + 8, 128 * k : 128 * k + 128] for k in range(pressure.shape[1] // 128)]
            for h in range(pressure.shape[0] // 8)
        ]
        loads[j] = lookup(every, panel[p]) * factor


def solve(pressure, panel, flags, diagonal, total, own, radial, around, cases):
    halves = cases // 8
    vm = pl.BlockSpec(memory_space=pltpu.VMEM)
    share = own // CASES
    ext_shape = (own + 2, radial, halves, 8, around)

    def field(n):
        return pltpu.VMEM((n, radial, halves, 8, around), jnp.float32)

    def wide(n):
        return pltpu.VMEM((n, radial, 1, 8, around), jnp.float32)

    def plain(n):
        return pltpu.VMEM((n, radial, around), jnp.float32)

    return pl.pallas_call(
        functools.partial(vcycle_kernel, total),
        out_shape=[
            jax.ShapeDtypeStruct((cases, own, radial, around), jnp.float32),
            jax.ShapeDtypeStruct(ext_shape, jnp.float32),
            jax.ShapeDtypeStruct((share, radial, pressure.shape[0] // 8, 8, around), jnp.float32),
            jax.ShapeDtypeStruct((share, radial, 1, 8, around), jnp.float32),
        ],
        in_specs=[vm] * 4,
        out_specs=[vm] * 4,
        scratch_shapes=[
            field(72), plain(72), field(72), field(72), field(72), wide(72), wide(72),
            field(36), plain(36), field(36), field(36), field(36), wide(36), wide(36),
            field(16), field(16), field(16), wide(16),
        ],
        compiler_params=pltpu.CompilerParams(vmem_limit_bytes=48 * 1024 * 1024),
        name="vcycle",
    )(pressure, panel, flags, diagonal)


def gram_kernel(ext, loads, chunk_diag, out, pieces, rows, along_z, along_y,
                piece_send, piece_recv, row_send, row_recv, z_send, z_recv, y_send, y_recv, own_sem):
    slab = lax.axis_index("slab")
    group = lax.axis_index("case")
    core = lax.rem(slab, CORES)
    z = lax.rem(slab // CORES, ZSIZE)
    y = slab // (CORES * ZSIZE)
    pair = slab - core
    share = loads.shape[0]
    barrier = pltpu.get_barrier_semaphore()

    mates = [(dx, dc) for dc in range(CORES) for dx in range(CASES) if (dx, dc) != (0, 0)]

    def mate(dx, dc):
        return (pair + lax.rem(core + dc, CORES), lax.rem(group + dx, CASES))

    def z_mate(d):
        return (y * (ZSIZE * CORES) + lax.rem(z + d, ZSIZE) * CORES + core, group)

    def y_mate(d):
        return (lax.rem(y + d, YSIZE) * (ZSIZE * CORES) + z * CORES + core, group)

    everyone = [mate(dx, dc) for dx, dc in mates]
    everyone += [z_mate(d) for d in range(1, ZSIZE)]
    everyone += [y_mate(d) for d in range(1, YSIZE)]
    for device in everyone:
        pl.semaphore_signal(barrier, inc=1, device_id=device, device_id_type=MESH)
    keep = pltpu.make_async_copy(ext.at[pl.ds(group * share, share + 2)], pieces.at[group], own_sem)
    keep.start()
    pl.semaphore_wait(barrier, len(everyone))

    copies = []
    for dx in (2, 1, 3):
        there = lax.rem(group + dx, CASES)
        copy = pltpu.make_async_remote_copy(
            src_ref=ext.at[pl.ds(there * share, share + 2)],
            dst_ref=pieces.at[group],
            send_sem=piece_send.at[there],
            recv_sem=piece_recv.at[group],
            device_id=(slab, there),
            device_id_type=MESH,
        )
        copy.start()
        copies.append(copy)
    keep.wait()
    for dx in (1, 2, 3):
        source = lax.rem(group + dx, CASES)
        pltpu.make_async_remote_copy(
            src_ref=pieces.at[source],
            dst_ref=pieces.at[source],
            send_sem=piece_send.at[source],
            recv_sem=piece_recv.at[source],
            device_id=(slab, source),
            device_id_type=MESH,
        ).wait_recv()

    radial, around = ext.shape[1], ext.shape[-1]
    image_parts, field_parts, load_parts = [], [], []
    for j in range(share):
        by_slot_image, by_slot_field = [], []
        for g in range(CASES):
            v = pieces[g, j + 1]
            near = pieces[g, j] + pieces[g, j + 2]
            by_slot_image.append(chunk_diag[j] * v - near - lateral(v))
            by_slot_field.append(v)
        for r in range(radial):
            image_parts.append(jnp.concatenate([v[r].reshape(-1, around) for v in by_slot_image], axis=0))
            field_parts.append(jnp.concatenate([v[r].reshape(-1, around) for v in by_slot_field], axis=0))
            load_parts.append(loads[j, r].reshape(-1, around))
    left = jnp.concatenate(
        [jnp.concatenate(image_parts, axis=1), jnp.concatenate(load_parts, axis=1)], axis=0
    )
    right = jnp.concatenate(field_parts, axis=1)
    product = lax.dot_general(
        left, right, (((1,), (1,)), ((), ())), precision=highest, preferred_element_type=jnp.float32
    )
    count = right.shape[0]
    both = jnp.concatenate([product[:count], product[count:]], axis=1)
    per = count // CASES
    me = group * CORES + core
    outgoing = rows.at[0]
    for g in range(CASES):
        rows[0, g] = both[g * per : (g + 1) * per]
    for dx, dc in mates:
        there_slab, there_group = mate(dx, dc)
        copy = pltpu.make_async_remote_copy(
            src_ref=rows.at[0, there_group],
            dst_ref=rows.at[1 + core, group],
            send_sem=row_send.at[dx, dc],
            recv_sem=row_recv.at[core, group],
            device_id=(there_slab, there_group),
            device_id_type=MESH,
        )
        copy.start()
        copies.append(copy)
    rows[1 + core, group] = rows[0, group]
    for dx, dc in mates:
        source_core, source_group = lax.rem(core + dc, CORES), lax.rem(group + dx, CASES)
        pltpu.make_async_remote_copy(
            src_ref=rows.at[1 + source_core, source_group],
            dst_ref=rows.at[1 + source_core, source_group],
            send_sem=row_send.at[dx, dc],
            recv_sem=row_recv.at[source_core, source_group],
            device_id=(slab, group),
            device_id_type=MESH,
        ).wait_recv()
    total = rows[1, 0]
    for c in range(CORES):
        for g in range(CASES):
            if (c, g) != (0, 0):
                total = total + rows[1 + c, g]

    def combine(total, slots, at, size, device, send, recv):
        slots[at] = total
        for d in range(1, size):
            copy = pltpu.make_async_remote_copy(
                src_ref=slots.at[at],
                dst_ref=slots.at[at],
                send_sem=send.at[d],
                recv_sem=recv.at[at],
                device_id=device(d),
                device_id_type=MESH,
            )
            copy.start()
            copies.append(copy)
        for d in range(1, size):
            source = lax.rem(at + d, size)
            pltpu.make_async_remote_copy(
                src_ref=slots.at[source],
                dst_ref=slots.at[source],
                send_sem=send.at[d],
                recv_sem=recv.at[source],
                device_id=device(d),
                device_id_type=MESH,
            ).wait_recv()
        result = slots[0]
        for d in range(1, size):
            result = result + slots[d]
        return result

    total = combine(total, along_z, z, ZSIZE, z_mate, z_send, z_recv)
    total = combine(total, along_y, y, YSIZE, y_mate, y_send, y_recv)
    out[...] = total
    for copy in copies:
        copy.wait_send()


def reduce_gram(ext, loads, chunk_diag, per):
    vm = pl.BlockSpec(memory_space=pltpu.VMEM)
    share = loads.shape[0]
    width = 2 * per * CASES
    return pl.pallas_call(
        gram_kernel,
        out_shape=jax.ShapeDtypeStruct((per, width), jnp.float32),
        in_specs=[vm] * 3,
        out_specs=vm,
        scratch_shapes=[
            pltpu.VMEM((CASES, share + 2) + ext.shape[1:], jnp.float32),
            pltpu.VMEM((1 + CORES, CASES, per, width), jnp.float32),
            pltpu.VMEM((ZSIZE, per, width), jnp.float32),
            pltpu.VMEM((YSIZE, per, width), jnp.float32),
            pltpu.SemaphoreType.DMA((CASES,)),
            pltpu.SemaphoreType.DMA((CASES,)),
            pltpu.SemaphoreType.DMA((CASES, CORES)),
            pltpu.SemaphoreType.DMA((CORES, CASES)),
            pltpu.SemaphoreType.DMA((ZSIZE,)),
            pltpu.SemaphoreType.DMA((ZSIZE,)),
            pltpu.SemaphoreType.DMA((YSIZE,)),
            pltpu.SemaphoreType.DMA((YSIZE,)),
            pltpu.SemaphoreType.DMA,
        ],
        compiler_params=pltpu.CompilerParams(collective_id=2, has_side_effects=True),
        name="gram",
    )(ext, loads, chunk_diag)


def local(pressure, panel, flags, diagonal):
    layers, radial, around = panel.shape
    slabs = lax.axis_size("slab")
    groups = lax.axis_size("case")
    per = pressure.shape[0] // groups
    total = layers * slabs
    spreads = exchange_halo(panel, flags, diagonal, slabs)
    wide = [x.reshape((-1,) + panel.shape[1:]) for x in spreads]
    fields, ext, loads, chunk_diag = solve(pressure, *wide, total, layers, radial, around, per)
    sums = reduce_gram(ext, loads, chunk_diag, per)
    scale = 1.0 / (total * radial * around)
    sums = sums * scale
    count = pressure.shape[0]
    return (fields, sums[:, :count], sums[:, count:])


def solution(mesh):
    in_specs = (P(), P("slab", None, None), P("slab", None, None), P("slab", None, None))
    out_specs = (P("case", "slab", None, None), P("case", None), P("case", None))
    return jax.shard_map(local, mesh=mesh, in_specs=in_specs, out_specs=out_specs, check_vma=False)
```

time: 731 us -> 94.4 us (0.13)
  blocking collectives: 492 us -> 0 us
  waiting for transfers between devices: 104 us -> 0 us
  Pallas kernels: 0 us -> 86.3 us
  starting transfers between devices: 75.5 us -> 0 us
  local copies, waits for them, and re-layouts: 29.9 us -> 6.44 us
  between operations: 14.9 us -> 0.66 us
    psum x1 -> x0, blocking collectives: 492 us -> none  [local(): gram_rows, cross_rows = lax.psum((gram_block, cross_block), 'slab')]
    pallas_call x0 -> x3, Pallas kernels: none -> 86.3 us  [the longest x1 37 us: solve(): pl.pallas_call(functools.partial(vcycle_kernel, total), out_shape=[jax.Sh...]
    ppermute x28 -> x0, starting transfers between devices: 75.5 us -> none  [the longest x12 39.6 us: with_halo(): lax.ppermute(tail, axis, [(i, (i + 1) % count) for i in range(ends)])]
    all_gather x1 -> x0, waiting for transfers between devices: 56.8 us -> none  [local(): piece = lax.all_gather(fields, 'case', axis=0, tiled=True)]
    ppermute x28 -> x0, waiting for transfers between devices: 47.6 us -> none  [the longest x12 38.7 us: with_halo(): lax.ppermute(head, axis, [((i + 1) % count, i) for i in range(ends)])]
    gather x2 -> x0, local copies, waits for them, and re-layouts: 23.3 us -> none  [local(): loads = jnp.take(case_rows, panel, axis=1) * span * keep]
  transfers between devices with their start and end apart: 29 -> 0, of which waited for: 16 -> 0; matrix products, arithmetic and copies ran while one was open for 1% -> 0% of each run, Pallas kernels for 0% -> 0%
where the time goes in v1:
time: 94.4 us; the launch traced here: 94.1 us
  Pallas kernels  86.3 us (91%)
  local copies, waits for them, and re-layouts  6.44 us (7%)
    pallas_call x1, Pallas kernels, solve(): pl.pallas_call(functools.partial(vcycle_kernel, total), out_shape=[jax.Sh...  37 us
    pallas_call x1, Pallas kernels, reduce_gram(): pl.pallas_call(gram_kernel, out_shape=jax.ShapeDtypeStruct((per, width),...  30.7 us
    pallas_call x1, Pallas kernels, exchange_halo(): pl.pallas_call(functools.partial(halo_kernel, slabs), out_shape=[jax.Shap...  18.6 us
    unnamed x14, local copies, waits for them, and re-layouts  5.76 us

profile of v1, /device:TPU:1, one launch (start us, length us, event | category | flops | bytes accessed | tf_op | source)
XLA Modules:
  0.0 94.1 jit_solution(16068073941383929702)
XLA Ops:
  0.6 18.6 %halo.1 = (s32[7,12,4,128]{3,2,1,0:T(4,128)}, s32[7,12,4,128]{3,2,1,0:T(4,128)}, f32[7,12,4,128]{3,2,1,0:T(4,128)}) custom-call(s32[12,4,128]{2,1,0:T(4,128)} %panel.1, s32[12,4,128]{2,1,0:T(4,128)} %flags.1, f32[12,4,128]{2,1,0:T(4,128)} %diagonal.1), custom_call_target="tpu_custom_call" | custom-call | tf_op jit(solution)/shard_map/halo/pallas_call | solution.py:59
  19.2 0.0 copy-start.2
  19.2 0.9 copy-done.2
  20.2 0.0 copy-start.3
  20.2 0.9 copy-done.3
  21.1 0.0 copy-start.4
  21.1 0.9 copy-done.4
  22.0 0.0 copy-start.5
  22.0 0.9 copy-done.5
  22.9 37.0 %vcycle.1 = (f32[16,12,4,128]{3,2,1,0:T(4,128)}, f32[14,4,2,8,128]{4,3,2,1,0:T(8,128)S(1)}, f32[3,4,8,8,128]{4,3,2,1,0:T(8,128)S(1)}, f32[3,4,1,8,128]{4,3,2,1,0:T(8,128)S(1)}) custom-call(f32[64,512]{1,0:T(8,128)S(1)} %copy-done.5, s32[84,4,128]{2,1,0:T(4,128)S(1)} %bitcast.3, s32[84,4,128]{2,1,0:T(4,128)S(1)} %bitcast.4, f32[84,4,128]{2,1,0:T(4,128)S(1)} %bitcast.5), custom_call_target="tpu_custom_call" | custom-call | tf_op jit(solution)/shard_map/vcycle/pallas_call | solution.py:256
  59.9 0.0 copy-start
  59.9 0.8 copy-done
  60.6 0.0 copy-start.1
  60.6 0.7 copy-done.1
  61.4 0.0 copy-start.6
  61.4 0.6 copy-done.6
  62.0 30.7 %gram.1 = f32[16,128]{1,0:T(8,128)} custom-call(f32[14,4,2,8,128]{4,3,2,1,0:T(8,128)} %copy-done, f32[3,4,8,8,128]{4,3,2,1,0:T(8,128)} %copy-done.1, f32[3,4,1,8,128]{4,3,2,1,0:T(8,128)} %copy-done.6), custom_call_target="tpu_custom_call" | custom-call | tf_op jit(solution)/shard_map/gram/pallas_call | solution.py:427
  92.7 0.7 broadcast_multiply_fusion
  93.4 0.7 fusion
Async XLA Ops:
  19.2 0.9 copy-start.2
  20.2 0.9 copy-start.3
  21.1 0.9 copy-start.4
  22.0 0.9 copy-start.5
  59.9 0.8 copy-start
  60.6 0.7 copy-start.1
  61.4 0.6 copy-start.6

commit v2 on v1

--- a/solution.py
+++ b/solution.py
@@ -14,6 +14,9 @@
 CASES = 4
 REACH = 3
 BASE = 29
+SETUP_STEP = 18
+SWEEP_STEP = 36
+COARSE_STEP = 11
 highest = lax.Precision.HIGHEST
 
 
@@ -78,123 +81,159 @@
 def lateral(v):
     flat = v.reshape(-1, v.shape[-1])
     sides = pltpu.roll(flat, 1, 1) + pltpu.roll(flat, flat.shape[1] - 1, 1)
-    edge = jnp.zeros_like(v[:1])
-    inward = jnp.concatenate([edge, v[:-1]], axis=0)
-    outward = jnp.concatenate([v[1:], edge], axis=0)
+    edge = jnp.zeros_like(v[:, :1])
+    inward = jnp.concatenate([edge, v[:, :-1]], axis=1)
+    outward = jnp.concatenate([v[:, 1:], edge], axis=1)
     return sides.reshape(v.shape) + (inward + outward)
 
 
 def spread(row):
-    return jnp.broadcast_to(row[:, None, None, :], (row.shape[0], 1, 8, row.shape[1]))
-
-
-def lookup(blocks, panel_row):
-    out = []
-    for r in range(panel_row.shape[0]):
-        where = jnp.broadcast_to(panel_row[r : r + 1], (8, panel_row.shape[1]))
-        low = where & 127
-        high = where >> 7
-        halves = []
-        for pieces in blocks:
-            found = jnp.take_along_axis(pieces[0], low, axis=1)
-            for j in range(1, len(pieces)):
-                found = jnp.where(high == j, jnp.take_along_axis(pieces[j], low, axis=1), found)
-            halves.append(found)
-        out.append(jnp.stack(halves))
-    return jnp.stack(out)
-
-
-def vcycle_kernel(total, pressure, panel, flags, diagonal, fields, ext, loads, chunk_diag,
-                  b0, c0, v0a, v0b, r0, w0, d0, b1, c1, v1a, v1b, r1, w1, d1, b2, v2a, v2b, w2):
+    return jnp.broadcast_to(row[:, :, None, None, :], row.shape[:2] + (1, 8, row.shape[2]))
+
+
+def lookup(blocks, panel_rows):
+    layers = []
+    for l in range(panel_rows.shape[0]):
+        out = []
+        for r in range(panel_rows.shape[1]):
+            where = jnp.broadcast_to(panel_rows[l, r : r + 1], (8, panel_rows.shape[2]))
+            low = where & 127
+            high = where >> 7
+            hits = [high == j for j in range(1, len(blocks[0]))]
+            halves = []
+            for pieces in blocks:
+                found = jnp.take_along_axis(pieces[0], low, axis=1)
+                for j in range(1, len(pieces)):
+                    found = jnp.where(hits[j - 1], jnp.take_along_axis(pieces[j], low, axis=1), found)
+                halves.append(found)
+            out.append(jnp.stack(halves))
+        layers.append(jnp.stack(out))
+    return jnp.stack(layers)
+
+
+def chunked(low, high, step, body):
+    whole = (high - low) // step
+
+    def run(k, _):
+        body(low, step * k, step)
+        return 0
+
+    lax.fori_loop(0, whole, run, 0)
+    rest = (high - low) - whole * step
+    if rest:
+        body(low, whole * step, rest)
+
+
+def vcycle_kernel(total, pressure_any, panel_any, flags_any, diagonal_any, fields, ext, loads, chunk_diag,
+                  pressure, panel, flags, diagonal, arrive, b0, c0, v0a, v0b, r0, w0, d0, b1, c1, v1a, v1b, r1, w1, d1, b2, v2a, v2b, w2):
     slab = lax.axis_index("slab")
     group = lax.axis_index("case")
     own = fields.shape[1]
     pad = REACH * own
     cases = fields.shape[0]
+    copies = [
+        pltpu.make_async_copy(src, dst, arrive.at[n])
+        for n, (src, dst) in enumerate(
+            ((pressure_any, pressure), (panel_any, panel), (flags_any, flags), (diagonal_any, diagonal))
+        )
+    ]
+    for copy in copies:
+        copy.start()
+    for copy in copies:
+        copy.wait()
     first = pl.multiple_of(group * cases, cases)
     blocks = [
         [pressure[pl.ds(first + 8 * h, 8), 128 * j : 128 * j + 128] for j in range(pressure.shape[1] // 128)]
         for h in range(cases // 8)
     ]
 
-    def inside(p, level):
-        g = p + slab * (own >> level)
+    def inside(p, shape, level):
+        g = lax.broadcasted_iota(jnp.int32, shape, 0) + (p + slab * (own >> level))
         return (g >= pad >> level) & (g < (total + pad) >> level)
 
-    def span_of(p):
-        at = (p + slab * own - pad).astype(jnp.float32)
+    def span_of(p, shape):
+        at = (lax.broadcasted_iota(jnp.int32, shape, 0) + (p + slab * own - pad)).astype(jnp.float32)
         return 1.0 + 2.0 * at / total
 
-    def setup(i, _):
-        p = i + (pad - BASE)
-        held = flags[p].astype(jnp.float32)
-        coeff = diagonal[p] + 4.0 * held
-        c0[i] = coeff
+    def setup(low, k, n):
+        p = k + (low + pad - BASE)
+        here = pl.ds(k + low, n)
+        held = flags[pl.ds(p, n)].astype(jnp.float32)
+        coeff = diagonal[pl.ds(p, n)] + 4.0 * held
+        c0[here] = coeff
         full = coeff + 6.0
-        within = inside(p, 0)
+        within = inside(p, full.shape, 0)
         w = spread(jnp.where(within, 0.7 / full, 0.0))
-        factor = spread(jnp.where(within, (1.0 - held) * span_of(p), 0.0))
-        w0[i] = w
-        d0[i] = spread(full)
-        rhs = lookup(blocks, panel[p]) * factor
-        b0[i] = rhs
-        v0a[i] = w * rhs
-        return 0
-
-    lax.fori_loop(0, 71, setup, 0)
+        factor = spread(jnp.where(within, (1.0 - held) * span_of(p, full.shape), 0.0))
+        w0[here] = w
+        d0[here] = spread(full)
+        rhs = lookup(blocks, panel[pl.ds(p, n)]) * factor
+        b0[here] = rhs
+        v0a[here] = w * rhs
+
+    chunked(0, 71, SETUP_STEP, setup)
+
+    def swept(src, rhs, w, weight, at, n):
+        wide = src[pl.ds(at - 1, n + 2)]
+        v = wide[1:-1]
+        near = wide[:-2] + wide[2:]
+        if weight != 1.0:
+            near = weight * near
+        return 0.3 * v + w[pl.ds(at, n)] * (rhs[pl.ds(at, n)] + near + lateral(v))
 
     def sweep(src, dst, rhs, w, weight, base, low, high):
-        def body(i, _):
-            v = src[i]
-            near = src[i - 1] + src[i + 1]
+        def body(start, k, n):
+            dst[pl.ds(k + start, n)] = swept(src, rhs, w, weight, k + start, n)
+
+        chunked(low + base, high + base, SWEEP_STEP, body)
+
+    def residual(src, dst, rhs, full, weight, base, low, high, level):
+        def body(start, k, n):
+            at = k + start
+            wide = src[pl.ds(at - 1, n + 2)]
+            v = wide[1:-1]
+            near = wide[:-2] + wide[2:]
             if weight != 1.0:
                 near = weight * near
-            dst[i] = 0.3 * v + w[i] * (rhs[i] + near + lateral(v))
-            return 0
-
-        lax.fori_loop(low + base, high + base, body, 0)
-
-    def residual(src, dst, rhs, full, weight, base, low, high, level):
-        def body(i, _):
-            v = src[i]
-            near = src[i - 1] + src[i + 1]
-            if weight != 1.0:
-                near = weight * near
-            left = rhs[i] - full[i] * v + (near + lateral(v))
-            dst[i] = jnp.where(inside(i + ((pad >> level) - base), level), left, 0.0)
-            return 0
-
-        lax.fori_loop(low + base, high + base, body, 0)
+            left = rhs[pl.ds(at, n)] - full[pl.ds(at, n)] * v + (near + lateral(v))
+            for j in range(n):
+                keep = inside(at + ((pad >> level) - base) + j, (1, 1, 1, 128), level)
+                dst[at + j] = jnp.where(keep, left[j], 0.0)
+
+        chunked(low + base, high + base, SWEEP_STEP, body)
 
     def restrict(fine, fine_base, cfine, rhs, ccoarse, w, full, vinit, weight, base, low, high, level):
-        def body(k, _):
-            at = 2 * k + (fine_base + 2 * low)
-            i = k + (low + base)
-            value = 0.5 * fine[at] + 0.25 * (fine[at + 1] + fine[at - 1])
-            coeff = 0.5 * (cfine[at] + cfine[at + 1])
-            diag = coeff + (2.0 * weight + 4.0)
-            if ccoarse is not None:
-                ccoarse[i] = coeff
-                full[i] = spread(diag)
-            scale = spread(jnp.where(inside(k + (low + (pad >> level)), level), 0.7 / diag, 0.0))
-            w[i] = scale
-            rhs[i] = value
-            vinit[i] = scale * value
-            return 0
-
-        lax.fori_loop(0, high - low, body, 0)
+        def body(start, k, n):
+            for j in range(n):
+                at = 2 * k + (fine_base + 2 * low + 2 * j)
+                i = k + (start + j)
+                value = 0.5 * fine[at] + 0.25 * (fine[at + 1] + fine[at - 1])
+                coeff = 0.5 * (cfine[at] + cfine[at + 1])
+                diag = coeff + (2.0 * weight + 4.0)
+                if ccoarse is not None:
+                    ccoarse[i] = coeff
+                    full[i] = spread(diag[None])[0]
+                keep = inside(k + (low + (pad >> level) + j), (1, 128), level)
+                scale = spread(jnp.where(keep, 0.7 / diag, 0.0)[None])[0]
+                w[i] = scale
+                rhs[i] = value
+                vinit[i] = scale * value
+
+        chunked(low + base, high + base, COARSE_STEP, body)
 
     def prolong(coarse, coarse_base, v, base, low, high, level):
-        def body(k, _):
-            here = coarse[k + (low + coarse_base)]
-            after = coarse[k + (low + coarse_base + 1)]
-            at = 2 * k + (2 * low + base)
-            p = 2 * k + (2 * low + (pad >> level))
-            v[at] = v[at] + jnp.where(inside(p, level), here, 0.0)
-            v[at + 1] = v[at + 1] + jnp.where(inside(p + 1, level), 0.5 * (here + after), 0.0)
-            return 0
-
-        lax.fori_loop(0, high - low, body, 0)
+        def body(start, k, n):
+            wide = coarse[pl.ds(k + start, n + 1)]
+            between = 0.5 * (wide[:-1] + wide[1:])
+            for j in range(n):
+                at = 2 * k + (2 * low + base + 2 * j)
+                p = 2 * k + (2 * low + (pad >> level) + 2 * j)
+                keep = inside(p, (1, 1, 1, 128), level)
+                v[at] = v[at] + jnp.where(keep, wide[j], 0.0)
+                keep = inside(p + 1, (1, 1, 1, 128), level)
+                v[at + 1] = v[at + 1] + jnp.where(keep, between[j], 0.0)
+
+        chunked(low + coarse_base, high + coarse_base, COARSE_STEP, body)
 
     sweep(v0a, v0b, b0, w0, 1.0, BASE, -28, 41)
     residual(v0b, r0, b0, d0, 1.0, BASE, -27, 40, 0)
@@ -209,40 +248,36 @@
     sweep(v1b, v1a, b1, w1, 0.25, 14, -3, 9)
     sweep(v1a, v1b, b1, w1, 0.25, 14, -2, 8)
     prolong(v1b, 14, v0b, BASE, -2, 7, 0)
-    even = v1b[7 + 14]
-    v0b[14 + BASE] = v0b[14 + BASE] + jnp.where(inside(14 + pad, 0), even, 0.0)
+    keep = inside(14 + pad, (1, 1, 1, 128), 0)
+    v0b[14 + BASE] = v0b[14 + BASE] + jnp.where(keep[0], v1b[7 + 14], 0.0)
     sweep(v0b, v0a, b0, w0, 1.0, BASE, -2, 14)
 
-    def last(k, _):
-        i = k + (BASE - 1)
-        v = v0a[i]
-        near = v0a[i - 1] + v0a[i + 1]
-        ext[k] = 0.3 * v + w0[i] * (b0[i] + near + lateral(v))
-        return 0
-
-    lax.fori_loop(0, own + 2, last, 0)
+    def last(start, k, n):
+        ext[pl.ds(k + start, n)] = swept(v0a, b0, w0, 1.0, k + (start + BASE), n)
+
+    chunked(0, own + 1, SWEEP_STEP, last)
     for f in range(own):
         for r in range(fields.shape[2]):
-            fields[:, f, r, :] = ext[f + 1, r].reshape(cases, 128)
+            fields[:, f, r, :] = ext[f, r].reshape(cases, 128)
 
     share = own // CASES
+    every = [
+        [pressure[8 * h : 8 * h + 8, 128 * k : 128 * k + 128] for k in range(pressure.shape[1] // 128)]
+        for h in range(pressure.shape[0] // 8)
+    ]
     for j in range(share):
         p = group * share + (pad + j)
-        held = flags[p].astype(jnp.float32)
-        factor = spread((1.0 - held) * span_of(p))
-        chunk_diag[j] = spread(diagonal[p] + 4.0 * held + 6.0)
-        every = [
-            [pressure[8 * h : 8 * h + 8, 128 * k : 128 * k + 128] for k in range(pressure.shape[1] // 128)]
-            for h in range(pressure.shape[0] // 8)
-        ]
-        loads[j] = lookup(every, panel[p]) * factor
+        held = flags[pl.ds(p, 1)].astype(jnp.float32)
+        factor = spread((1.0 - held) * span_of(p, held.shape))
+        chunk_diag[pl.ds(j, 1)] = spread(diagonal[pl.ds(p, 1)] + 4.0 * held + 6.0)
+        loads[pl.ds(j, 1)] = lookup(every, panel[pl.ds(p, 1)]) * factor
 
 
 def solve(pressure, panel, flags, diagonal, total, own, radial, around, cases):
     halves = cases // 8
     vm = pl.BlockSpec(memory_space=pltpu.VMEM)
     share = own // CASES
-    ext_shape = (own + 2, radial, halves, 8, around)
+    ext_shape = (own + 1, radial, halves, 8, around)
 
     def field(n):
         return pltpu.VMEM((n, radial, halves, 8, around), jnp.float32)
@@ -261,19 +296,24 @@
             jax.ShapeDtypeStruct((share, radial, pressure.shape[0] // 8, 8, around), jnp.float32),
             jax.ShapeDtypeStruct((share, radial, 1, 8, around), jnp.float32),
         ],
-        in_specs=[vm] * 4,
+        in_specs=[pl.BlockSpec(memory_space=pl.ANY)] * 4,
         out_specs=[vm] * 4,
         scratch_shapes=[
+            pltpu.VMEM(pressure.shape, jnp.float32),
+            pltpu.VMEM(panel.shape, jnp.int32),
+            pltpu.VMEM(panel.shape, jnp.int32),
+            pltpu.VMEM(panel.shape, jnp.float32),
+            pltpu.SemaphoreType.DMA((4,)),
             field(72), plain(72), field(72), field(72), field(72), wide(72), wide(72),
             field(36), plain(36), field(36), field(36), field(36), wide(36), wide(36),
             field(16), field(16), field(16), wide(16),
         ],
-        compiler_params=pltpu.CompilerParams(vmem_limit_bytes=48 * 1024 * 1024),
+        compiler_params=pltpu.CompilerParams(vmem_limit_bytes=64000000),
         name="vcycle",
     )(pressure, panel, flags, diagonal)
 
 
-def gram_kernel(ext, loads, chunk_diag, out, pieces, rows, along_z, along_y,
+def gram_kernel(ext, loads_any, diag_any, gram, cross, loads, chunk_diag, pieces, rows, along_z, along_y,
                 piece_send, piece_recv, row_send, row_recv, z_send, z_recv, y_send, y_recv, own_sem):
     slab = lax.axis_index("slab")
     group = lax.axis_index("case")
@@ -300,15 +340,19 @@
     everyone += [y_mate(d) for d in range(1, YSIZE)]
     for device in everyone:
         pl.semaphore_signal(barrier, inc=1, device_id=device, device_id_type=MESH)
-    keep = pltpu.make_async_copy(ext.at[pl.ds(group * share, share + 2)], pieces.at[group], own_sem)
+    keep = pltpu.make_async_copy(ext.at[pl.ds(group * share, share + 1)], pieces.at[group], own_sem.at[0])
     keep.start()
+    load_copy = pltpu.make_async_copy(loads_any, loads, own_sem.at[1])
+    load_copy.start()
+    diag_copy = pltpu.make_async_copy(diag_any, chunk_diag, own_sem.at[2])
+    diag_copy.start()
     pl.semaphore_wait(barrier, len(everyone))
 
     copies = []
     for dx in (2, 1, 3):
         there = lax.rem(group + dx, CASES)
         copy = pltpu.make_async_remote_copy(
-            src_ref=ext.at[pl.ds(there * share, share + 2)],
+            src_ref=ext.at[pl.ds(there * share, share + 1)],
             dst_ref=pieces.at[group],
             send_sem=piece_send.at[there],
             recv_sem=piece_recv.at[group],
@@ -318,6 +362,8 @@
         copy.start()
         copies.append(copy)
     keep.wait()
+    load_copy.wait()
+    diag_copy.wait()
     for dx in (1, 2, 3):
         source = lax.rem(group + dx, CASES)
         pltpu.make_async_remote_copy(
@@ -330,30 +376,33 @@
         ).wait_recv()
 
     radial, around = ext.shape[1], ext.shape[-1]
-    image_parts, field_parts, load_parts = [], [], []
+    image_parts, field_parts, above_parts, load_parts = [], [], [], []
+
+    def rows_of(values, r):
+        return jnp.concatenate([v[0, r].reshape(-1, around) for v in values], axis=0)
+
     for j in range(share):
-        by_slot_image, by_slot_field = [], []
-        for g in range(CASES):
-            v = pieces[g, j + 1]
-            near = pieces[g, j] + pieces[g, j + 2]
-            by_slot_image.append(chunk_diag[j] * v - near - lateral(v))
-            by_slot_field.append(v)
+        here = [pieces[g, j : j + 1] for g in range(CASES)]
+        above = [pieces[g, j + 1 : j + 2] for g in range(CASES)]
+        image = [chunk_diag[j : j + 1] * v - lateral(v) for v in here]
         for r in range(radial):
-            image_parts.append(jnp.concatenate([v[r].reshape(-1, around) for v in by_slot_image], axis=0))
-            field_parts.append(jnp.concatenate([v[r].reshape(-1, around) for v in by_slot_field], axis=0))
+            image_parts.append(rows_of(image, r))
+            field_parts.append(rows_of(here, r))
+            above_parts.append(rows_of(above, r))
             load_parts.append(loads[j, r].reshape(-1, around))
     left = jnp.concatenate(
-        [jnp.concatenate(image_parts, axis=1), jnp.concatenate(load_parts, axis=1)], axis=0
+        [jnp.concatenate(parts, axis=1) for parts in (image_parts, above_parts, load_parts)], axis=0
     )
     right = jnp.concatenate(field_parts, axis=1)
     product = lax.dot_general(
         left, right, (((1,), (1,)), ((), ())), precision=highest, preferred_element_type=jnp.float32
     )
     count = right.shape[0]
-    both = jnp.concatenate([product[:count], product[count:]], axis=1)
+    coupling = product[count : 2 * count]
+    both = jnp.concatenate(
+        [product[:count] - (coupling + coupling.T), product[2 * count :]], axis=1
+    )
     per = count // CASES
-    me = group * CORES + core
-    outgoing = rows.at[0]
     for g in range(CASES):
         rows[0, g] = both[g * per : (g + 1) * per]
     for dx, dc in mates:
@@ -415,7 +464,8 @@
 
     total = combine(total, along_z, z, ZSIZE, z_mate, z_send, z_recv)
     total = combine(total, along_y, y, YSIZE, y_mate, y_send, y_recv)
-    out[...] = total
+    gram[...] = total[:, :count]
+    cross[...] = total[:, count:]
     for copy in copies:
         copy.wait_send()
 
@@ -426,11 +476,13 @@
     width = 2 * per * CASES
     return pl.pallas_call(
         gram_kernel,
-        out_shape=jax.ShapeDtypeStruct((per, width), jnp.float32),
-        in_specs=[vm] * 3,
-        out_specs=vm,
+        out_shape=[jax.ShapeDtypeStruct((per, width // 2), jnp.float32)] * 2,
+        in_specs=[pl.BlockSpec(memory_space=pl.ANY)] * 3,
+        out_specs=[vm] * 2,
         scratch_shapes=[
-            pltpu.VMEM((CASES, share + 2) + ext.shape[1:], jnp.float32),
+            pltpu.VMEM(loads.shape, jnp.float32),
+            pltpu.VMEM(chunk_diag.shape, jnp.float32),
+            pltpu.VMEM((CASES, share + 1) + ext.shape[1:], jnp.float32),
             pltpu.VMEM((1 + CORES, CASES, per, width), jnp.float32),
             pltpu.VMEM((ZSIZE, per, width), jnp.float32),
             pltpu.VMEM((YSIZE, per, width), jnp.float32),
@@ -442,9 +494,9 @@
             pltpu.SemaphoreType.DMA((ZSIZE,)),
             pltpu.SemaphoreType.DMA((YSIZE,)),
             pltpu.SemaphoreType.DMA((YSIZE,)),
-            pltpu.SemaphoreType.DMA,
+            pltpu.SemaphoreType.DMA((3,)),
         ],
-        compiler_params=pltpu.CompilerParams(collective_id=2, has_side_effects=True),
+        compiler_params=pltpu.CompilerParams(collective_id=2, has_side_effects=True, vmem_limit_bytes=64000000),
         name="gram",
     )(ext, loads, chunk_diag)
 
@@ -458,11 +510,9 @@
     spreads = exchange_halo(panel, flags, diagonal, slabs)
     wide = [x.reshape((-1,) + panel.shape[1:]) for x in spreads]
     fields, ext, loads, chunk_diag = solve(pressure, *wide, total, layers, radial, around, per)
-    sums = reduce_gram(ext, loads, chunk_diag, per)
+    gram, cross = reduce_gram(ext, loads, chunk_diag, per)
     scale = 1.0 / (total * radial * around)
-    sums = sums * scale
-    count = pressure.shape[0]
-    return (fields, sums[:, :count], sums[:, count:])
+    return (fields, gram * scale, cross * scale)
 
 
 def solution(mesh):

time: 94.4 us -> 61.5 us (0.65)
  Pallas kernels: 86.3 us -> 59.3 us
  local copies, waits for them, and re-layouts: 6.44 us -> 0 us
    pallas_call x1, Pallas kernels: 37 us -> 11.8 us  [solve(): pl.pallas_call(functools.partial(vcycle_kernel, total), out_shape=[jax.Sh...]
    unnamed x14 -> x0, local copies, waits for them, and re-layouts: 5.76 us -> none
    pallas_call x1, Pallas kernels: 30.7 us -> 28.9 us  [reduce_gram(): pl.pallas_call(gram_kernel, out_shape=[jax.ShapeDtypeStruct((per, width /...]
where the time goes in v2:
time: 61.5 us; the launch traced here: 61.3 us
  Pallas kernels  59.3 us (96%)
  other arithmetic  1.32 us (2%)
  between operations  0.65 us (1%)
    pallas_call x1, Pallas kernels, reduce_gram(): pl.pallas_call(gram_kernel, out_shape=[jax.ShapeDtypeStruct((per, width /...  28.9 us
    pallas_call x1, Pallas kernels, exchange_halo(): pl.pallas_call(functools.partial(halo_kernel, slabs), out_shape=[jax.Shap...  18.6 us
    pallas_call x1, Pallas kernels, solve(): pl.pallas_call(functools.partial(vcycle_kernel, total), out_shape=[jax.Sh...  11.8 us
    mul x1, other arithmetic, local(): return (fields, gram * scale, cross * scale)  1.32 us

profile of v2, /device:TPU:1, one launch (start us, length us, event | category | flops | bytes accessed | tf_op | source)
XLA Modules:
  0.0 61.3 jit_solution(2069522461165454786)
XLA Ops:
  0.6 18.6 %halo.1 = (s32[7,12,4,128]{3,2,1,0:T(4,128)}, s32[7,12,4,128]{3,2,1,0:T(4,128)}, f32[7,12,4,128]{3,2,1,0:T(4,128)}) custom-call(s32[12,4,128]{2,1,0:T(4,128)} %panel.1, s32[12,4,128]{2,1,0:T(4,128)} %flags.1, f32[12,4,128]{2,1,0:T(4,128)} %diagonal.1), custom_call_target="tpu_custom_call" | custom-call | tf_op jit(solution)/shard_map/halo/pallas_call | solution.py:62
  19.2 11.8 %vcycle.1 = (f32[16,12,4,128]{3,2,1,0:T(4,128)}, f32[13,4,2,8,128]{4,3,2,1,0:T(8,128)}, f32[3,4,8,8,128]{4,3,2,1,0:T(8,128)}, f32[3,4,1,8,128]{4,3,2,1,0:T(8,128)}) custom-call(f32[64,512]{1,0:T(8,128)} %pressure_any.1, s32[84,4,128]{2,1,0:T(4,128)} %bitcast.3, s32[84,4,128]{2,1,0:T(4,128)} %bitcast.4, f32[84,4,128]{2,1,0:T(4,128)} %bitcast.5), custom_call_target="tpu_custom_call" | custom-call | tf_op jit(solution)/shard_map/vcycle/pallas_call | solution.py:291
  31.0 28.9 %gram.1 = (f32[16,64]{1,0:T(8,128)}, f32[16,64]{1,0:T(8,128)}) custom-call(f32[13,4,2,8,128]{4,3,2,1,0:T(8,128)} %get-tuple-element.16.ext, f32[3,4,8,8,128]{4,3,2,1,0:T(8,128)} %get-tuple-element.17.loads_any, f32[3,4,1,8,128]{4,3,2,1,0:T(8,128)} %get-tuple-element.18.diag_any), custom_call_target="tpu_custom_call" | custom-call | tf_op jit(solution)/shard_map/gram/pallas_call | solution.py:477
  60.0 1.3 %broadcast_multiply_fusion = (f32[16,64]{1,0:T(8,128)}, f32[16,64]{1,0:T(8,128)}) fusion(f32[16,64]{1,0:T(8,128)} %get-tuple-element.20, f32[16,64]{1,0:T(8,128)} %get-tuple-element.19), kind=kLoop, calls=%fused_computation | loop fusion | flops 2048 | bytes 16384 | tf_op jit(solution)/shard_map/mul | solution.py:515

commit v3 on v2

--- a/solution.py
+++ b/solution.py
@@ -124,13 +124,38 @@
         body(low, whole * step, rest)
 
 
-def vcycle_kernel(total, pressure_any, panel_any, flags_any, diagonal_any, fields, ext, loads, chunk_diag,
-                  pressure, panel, flags, diagonal, arrive, b0, c0, v0a, v0b, r0, w0, d0, b1, c1, v1a, v1b, r1, w1, d1, b2, v2a, v2b, w2):
+def step_kernel(total, pressure_any, panel_any, flags_any, diagonal_any, fields_any, gram, cross,
+                fields, field_sem, loads, chunk_diag, pieces, rows, along_z, along_y,
+                piece_send, piece_recv, row_send, row_recv, z_send, z_recv, y_send, y_recv, own_sem,
+                ext, pressure, panel, flags, diagonal, arrive, b0, c0, v0a, v0b, r0, w0, d0, b1, c1, v1a, v1b, r1, w1, d1, b2, v2a, v2b, w2):
     slab = lax.axis_index("slab")
     group = lax.axis_index("case")
     own = fields.shape[1]
     pad = REACH * own
     cases = fields.shape[0]
+    core = lax.rem(slab, CORES)
+    z = lax.rem(slab // CORES, ZSIZE)
+    y = slab // (CORES * ZSIZE)
+    pair = slab - core
+    share = loads.shape[0]
+    barrier = pltpu.get_barrier_semaphore()
+
+    mates = [(dx, dc) for dc in range(CORES) for dx in range(CASES) if (dx, dc) != (0, 0)]
+
+    def mate(dx, dc):
+        return (pair + lax.rem(core + dc, CORES), lax.rem(group + dx, CASES))
+
+    def z_mate(d):
+        return (y * (ZSIZE * CORES) + lax.rem(z + d, ZSIZE) * CORES + core, group)
+
+    def y_mate(d):
+        return (lax.rem(y + d, YSIZE) * (ZSIZE * CORES) + z * CORES + core, group)
+
+    everyone = [mate(dx, dc) for dx, dc in mates]
+    everyone += [z_mate(d) for d in range(1, ZSIZE)]
+    everyone += [y_mate(d) for d in range(1, YSIZE)]
+    for device in everyone:
+        pl.semaphore_signal(barrier, inc=1, device_id=device, device_id_type=MESH)
     copies = [
         pltpu.make_async_copy(src, dst, arrive.at[n])
         for n, (src, dst) in enumerate(
@@ -256,99 +281,10 @@
         ext[pl.ds(k + start, n)] = swept(v0a, b0, w0, 1.0, k + (start + BASE), n)
 
     chunked(0, own + 1, SWEEP_STEP, last)
-    for f in range(own):
-        for r in range(fields.shape[2]):
-            fields[:, f, r, :] = ext[f, r].reshape(cases, 128)
-
-    share = own // CASES
-    every = [
-        [pressure[8 * h : 8 * h + 8, 128 * k : 128 * k + 128] for k in range(pressure.shape[1] // 128)]
-        for h in range(pressure.shape[0] // 8)
-    ]
-    for j in range(share):
-        p = group * share + (pad + j)
-        held = flags[pl.ds(p, 1)].astype(jnp.float32)
-        factor = spread((1.0 - held) * span_of(p, held.shape))
-        chunk_diag[pl.ds(j, 1)] = spread(diagonal[pl.ds(p, 1)] + 4.0 * held + 6.0)
-        loads[pl.ds(j, 1)] = lookup(every, panel[pl.ds(p, 1)]) * factor
-
-
-def solve(pressure, panel, flags, diagonal, total, own, radial, around, cases):
-    halves = cases // 8
-    vm = pl.BlockSpec(memory_space=pltpu.VMEM)
-    share = own // CASES
-    ext_shape = (own + 1, radial, halves, 8, around)
-
-    def field(n):
-        return pltpu.VMEM((n, radial, halves, 8, around), jnp.float32)
-
-    def wide(n):
-        return pltpu.VMEM((n, radial, 1, 8, around), jnp.float32)
-
-    def plain(n):
-        return pltpu.VMEM((n, radial, around), jnp.float32)
-
-    return pl.pallas_call(
-        functools.partial(vcycle_kernel, total),
-        out_shape=[
-            jax.ShapeDtypeStruct((cases, own, radial, around), jnp.float32),
-            jax.ShapeDtypeStruct(ext_shape, jnp.float32),
-            jax.ShapeDtypeStruct((share, radial, pressure.shape[0] // 8, 8, around), jnp.float32),
-            jax.ShapeDtypeStruct((share, radial, 1, 8, around), jnp.float32),
-        ],
-        in_specs=[pl.BlockSpec(memory_space=pl.ANY)] * 4,
-        out_specs=[vm] * 4,
-        scratch_shapes=[
-            pltpu.VMEM(pressure.shape, jnp.float32),
-            pltpu.VMEM(panel.shape, jnp.int32),
-            pltpu.VMEM(panel.shape, jnp.int32),
-            pltpu.VMEM(panel.shape, jnp.float32),
-            pltpu.SemaphoreType.DMA((4,)),
-            field(72), plain(72), field(72), field(72), field(72), wide(72), wide(72),
-            field(36), plain(36), field(36), field(36), field(36), wide(36), wide(36),
-            field(16), field(16), field(16), wide(16),
-        ],
-        compiler_params=pltpu.CompilerParams(vmem_limit_bytes=64000000),
-        name="vcycle",
-    )(pressure, panel, flags, diagonal)
-
-
-def gram_kernel(ext, loads_any, diag_any, gram, cross, loads, chunk_diag, pieces, rows, along_z, along_y,
-                piece_send, piece_recv, row_send, row_recv, z_send, z_recv, y_send, y_recv, own_sem):
-    slab = lax.axis_index("slab")
-    group = lax.axis_index("case")
-    core = lax.rem(slab, CORES)
-    z = lax.rem(slab // CORES, ZSIZE)
-    y = slab // (CORES * ZSIZE)
-    pair = slab - core
-    share = loads.shape[0]
-    barrier = pltpu.get_barrier_semaphore()
-
-    mates = [(dx, dc) for dc in range(CORES) for dx in range(CASES) if (dx, dc) != (0, 0)]
-
-    def mate(dx, dc):
-        return (pair + lax.rem(core + dc, CORES), lax.rem(group + dx, CASES))
-
-    def z_mate(d):
-        return (y * (ZSIZE * CORES) + lax.rem(z + d, ZSIZE) * CORES + core, group)
-
-    def y_mate(d):
-        return (lax.rem(y + d, YSIZE) * (ZSIZE * CORES) + z * CORES + core, group)
-
-    everyone = [mate(dx, dc) for dx, dc in mates]
-    everyone += [z_mate(d) for d in range(1, ZSIZE)]
-    everyone += [y_mate(d) for d in range(1, YSIZE)]
-    for device in everyone:
-        pl.semaphore_signal(barrier, inc=1, device_id=device, device_id_type=MESH)
-    keep = pltpu.make_async_copy(ext.at[pl.ds(group * share, share + 1)], pieces.at[group], own_sem.at[0])
+    keep = pltpu.make_async_copy(ext.at[pl.ds(group * share, share + 1)], pieces.at[group], own_sem)
     keep.start()
-    load_copy = pltpu.make_async_copy(loads_any, loads, own_sem.at[1])
-    load_copy.start()
-    diag_copy = pltpu.make_async_copy(diag_any, chunk_diag, own_sem.at[2])
-    diag_copy.start()
     pl.semaphore_wait(barrier, len(everyone))
-
-    copies = []
+    sent = []
     for dx in (2, 1, 3):
         there = lax.rem(group + dx, CASES)
         copy = pltpu.make_async_remote_copy(
@@ -360,10 +296,25 @@
             device_id_type=MESH,
         )
         copy.start()
-        copies.append(copy)
+        sent.append(copy)
+    for f in range(own):
+        for r in range(fields.shape[2]):
+            fields[:, f, r, :] = ext[f, r].reshape(cases, 128)
+
+    field_copy = pltpu.make_async_copy(fields, fields_any, field_sem)
+    field_copy.start()
+    every = [
+        [pressure[8 * h : 8 * h + 8, 128 * k : 128 * k + 128] for k in range(pressure.shape[1] // 128)]
+        for h in range(pressure.shape[0] // 8)
+    ]
+    for j in range(share):
+        p = group * share + (pad + j)
+        held = flags[pl.ds(p, 1)].astype(jnp.float32)
+        factor = spread((1.0 - held) * span_of(p, held.shape))
+        chunk_diag[pl.ds(j, 1)] = spread(diagonal[pl.ds(p, 1)] + 4.0 * held + 6.0)
+        loads[pl.ds(j, 1)] = lookup(every, panel[pl.ds(p, 1)]) * factor
+
     keep.wait()
-    load_copy.wait()
-    diag_copy.wait()
     for dx in (1, 2, 3):
         source = lax.rem(group + dx, CASES)
         pltpu.make_async_remote_copy(
@@ -416,7 +367,7 @@
             device_id_type=MESH,
         )
         copy.start()
-        copies.append(copy)
+        sent.append(copy)
     rows[1 + core, group] = rows[0, group]
     for dx, dc in mates:
         source_core, source_group = lax.rem(core + dc, CORES), lax.rem(group + dx, CASES)
@@ -446,7 +397,7 @@
                 device_id_type=MESH,
             )
             copy.start()
-            copies.append(copy)
+            sent.append(copy)
         for d in range(1, size):
             source = lax.rem(at + d, size)
             pltpu.make_async_remote_copy(
@@ -466,26 +417,45 @@
     total = combine(total, along_y, y, YSIZE, y_mate, y_send, y_recv)
     gram[...] = total[:, :count]
     cross[...] = total[:, count:]
-    for copy in copies:
+    for copy in sent:
         copy.wait_send()
-
-
-def reduce_gram(ext, loads, chunk_diag, per):
+    field_copy.wait()
+
+
+def solve(pressure, panel, flags, diagonal, total, own, radial, around, cases):
+    halves = cases // 8
+    share = own // CASES
+    width = 2 * cases * CASES
+    anyspace = pl.BlockSpec(memory_space=pl.ANY)
     vm = pl.BlockSpec(memory_space=pltpu.VMEM)
-    share = loads.shape[0]
-    width = 2 * per * CASES
+
+    def field(n):
+        return pltpu.VMEM((n, radial, halves, 8, around), jnp.float32)
+
+    def wide(n):
+        return pltpu.VMEM((n, radial, 1, 8, around), jnp.float32)
+
+    def plain(n):
+        return pltpu.VMEM((n, radial, around), jnp.float32)
+
     return pl.pallas_call(
-        gram_kernel,
-        out_shape=[jax.ShapeDtypeStruct((per, width // 2), jnp.float32)] * 2,
-        in_specs=[pl.BlockSpec(memory_space=pl.ANY)] * 3,
-        out_specs=[vm] * 2,
+        functools.partial(step_kernel, total),
+        out_shape=[
+            jax.ShapeDtypeStruct((cases, own, radial, around), jnp.float32),
+            jax.ShapeDtypeStruct((cases, width // 2), jnp.float32),
+            jax.ShapeDtypeStruct((cases, width // 2), jnp.float32),
+        ],
+        in_specs=[anyspace] * 4,
+        out_specs=[anyspace, vm, vm],
         scratch_shapes=[
-            pltpu.VMEM(loads.shape, jnp.float32),
-            pltpu.VMEM(chunk_diag.shape, jnp.float32),
-            pltpu.VMEM((CASES, share + 1) + ext.shape[1:], jnp.float32),
-            pltpu.VMEM((1 + CORES, CASES, per, width), jnp.float32),
-            pltpu.VMEM((ZSIZE, per, width), jnp.float32),
-            pltpu.VMEM((YSIZE, per, width), jnp.float32),
+            pltpu.VMEM((cases, own, radial, around), jnp.float32),
+            pltpu.SemaphoreType.DMA,
+            pltpu.VMEM((share, radial, pressure.shape[0] // 8, 8, around), jnp.float32),
+            wide(share),
+            pltpu.VMEM((CASES, share + 1, radial, halves, 8, around), jnp.float32),
+            pltpu.VMEM((1 + CORES, CASES, cases, width), jnp.float32),
+            pltpu.VMEM((ZSIZE, cases, width), jnp.float32),
+            pltpu.VMEM((YSIZE, cases, width), jnp.float32),
             pltpu.SemaphoreType.DMA((CASES,)),
             pltpu.SemaphoreType.DMA((CASES,)),
             pltpu.SemaphoreType.DMA((CASES, CORES)),
@@ -494,11 +464,22 @@
             pltpu.SemaphoreType.DMA((ZSIZE,)),
             pltpu.SemaphoreType.DMA((YSIZE,)),
             pltpu.SemaphoreType.DMA((YSIZE,)),
-            pltpu.SemaphoreType.DMA((3,)),
+            pltpu.SemaphoreType.DMA,
+            field(own + 1),
+            pltpu.VMEM(pressure.shape, jnp.float32),
+            pltpu.VMEM(panel.shape, jnp.int32),
+            pltpu.VMEM(panel.shape, jnp.int32),
+            pltpu.VMEM(panel.shape, jnp.float32),
+            pltpu.SemaphoreType.DMA((4,)),
+            field(72), plain(72), field(72), field(72), field(72), wide(72), wide(72),
+            field(36), plain(36), field(36), field(36), field(36), wide(36), wide(36),
+            field(16), field(16), field(16), wide(16),
         ],
-        compiler_params=pltpu.CompilerParams(collective_id=2, has_side_effects=True, vmem_limit_bytes=64000000),
-        name="gram",
-    )(ext, loads, chunk_diag)
+        compiler_params=pltpu.CompilerParams(
+            collective_id=2, has_side_effects=True, vmem_limit_bytes=64000000
+        ),
+        name="step",
+    )(pressure, panel, flags, diagonal)
 
 
 def local(pressure, panel, flags, diagonal):
@@ -509,8 +490,7 @@
     total = layers * slabs
     spreads = exchange_halo(panel, flags, diagonal, slabs)
     wide = [x.reshape((-1,) + panel.shape[1:]) for x in spreads]
-    fields, ext, loads, chunk_diag = solve(pressure, *wide, total, layers, radial, around, per)
-    gram, cross = reduce_gram(ext, loads, chunk_diag, per)
+    fields, gram, cross = solve(pressure, *wide, total, layers, radial, around, per)
     scale = 1.0 / (total * radial * around)
     return (fields, gram * scale, cross * scale)
 

time: 61.5 us -> 58.7 us (0.954)
  Pallas kernels: 59.3 us -> 54.7 us
  local copies, waits for them, and re-layouts: 0 us -> 1.77 us
    pallas_call x2 -> x1, Pallas kernels: 40.7 us -> 36.1 us  [solve(): pl.pallas_call(functools.partial(step_kernel, total), out_shape=[jax.Shap...]
    unnamed x0 -> x1, local copies, waits for them, and re-layouts: none -> 1.77 us
where the time goes in v3:
time: 58.7 us; the launch traced here: 58.5 us
  Pallas kernels  54.7 us (93%)
  local copies, waits for them, and re-layouts  1.77 us (3%)
  other arithmetic  1.32 us (2%)
  between operations  0.65 us (1%)
    pallas_call x1, Pallas kernels, solve(): pl.pallas_call(functools.partial(step_kernel, total), out_shape=[jax.Shap...  36.1 us
    pallas_call x1, Pallas kernels, exchange_halo(): pl.pallas_call(functools.partial(halo_kernel, slabs), out_shape=[jax.Shap...  18.6 us
    unnamed x1, local copies, waits for them, and re-layouts  1.77 us
    mul x1, other arithmetic, local(): return (fields, gram * scale, cross * scale)  1.32 us

profile of v3, /device:TPU:1, one launch (start us, length us, event | category | flops | bytes accessed | tf_op | source)
XLA Modules:
  0.0 58.5 jit_solution(9662313368041963844)
XLA Ops:
  0.6 18.6 %halo.1 = (s32[7,12,4,128]{3,2,1,0:T(4,128)}, s32[7,12,4,128]{3,2,1,0:T(4,128)}, f32[7,12,4,128]{3,2,1,0:T(4,128)}) custom-call(s32[12,4,128]{2,1,0:T(4,128)} %panel.1, s32[12,4,128]{2,1,0:T(4,128)} %flags.1, f32[12,4,128]{2,1,0:T(4,128)} %diagonal.1), custom_call_target="tpu_custom_call" | custom-call | tf_op jit(solution)/shard_map/halo/pallas_call | solution.py:62
  19.2 36.1 %step.1 = (f32[16,12,4,128]{3,2,1,0:T(4,128)}, f32[16,64]{1,0:T(8,128)}, f32[16,64]{1,0:T(8,128)}) custom-call(f32[64,512]{1,0:T(8,128)} %pressure_any.1, s32[84,4,128]{2,1,0:T(4,128)} %bitcast.3, s32[84,4,128]{2,1,0:T(4,128)} %bitcast.4, f32[84,4,128]{2,1,0:T(4,128)} %bitcast.5), custom_call_target="tpu_custom_call" | custom-call | tf_op jit(solution)/shard_map/step/pallas_call | solution.py:441
  55.4 1.3 %broadcast_multiply_fusion = (f32[16,64]{1,0:T(8,128)}, f32[16,64]{1,0:T(8,128)}) fusion(f32[16,64]{1,0:T(8,128)} %get-tuple-element.14, f32[16,64]{1,0:T(8,128)} %get-tuple-element.13), kind=kLoop, calls=%fused_computation | loop fusion | flops 2048 | bytes 16384 | tf_op jit(solution)/shard_map/mul | solution.py:495
  56.7 1.8 %copy.8 = f32[16,12,4,128]{3,2,1,0:T(4,128)} copy(f32[16,12,4,128]{3,2,1,0:T(4,128)} %get-tuple-element.20) | data formatting | bytes 786432

commit v4 on v3

--- a/solution.py
+++ b/solution.py
@@ -126,7 +126,7 @@
 
 def step_kernel(total, pressure_any, panel_any, flags_any, diagonal_any, fields_any, gram, cross,
                 fields, field_sem, loads, chunk_diag, pieces, rows, along_z, along_y,
-                piece_send, piece_recv, row_send, row_recv, z_send, z_recv, y_send, y_recv, own_sem,
+                relay, relay_sems, piece_send, piece_recv, row_send, row_recv, z_send, z_recv, y_send, y_recv, own_sem,
                 ext, pressure, panel, flags, diagonal, arrive, b0, c0, v0a, v0b, r0, w0, d0, b1, c1, v1a, v1b, r1, w1, d1, b2, v2a, v2b, w2):
     slab = lax.axis_index("slab")
     group = lax.axis_index("case")
@@ -285,7 +285,22 @@
     keep.start()
     pl.semaphore_wait(barrier, len(everyone))
     sent = []
-    for dx in (2, 1, 3):
+    passed = []
+    half = (share + 1) // 2
+    spans = ((0, half), (half, share + 1 - half))
+    across = lax.rem(group + 2, CASES)
+    for way, (start, many) in enumerate(spans):
+        copy = pltpu.make_async_remote_copy(
+            src_ref=ext.at[pl.ds(across * share + start, many)],
+            dst_ref=relay.at[way, pl.ds(0, many)],
+            send_sem=relay_sems.at[0, way],
+            recv_sem=relay_sems.at[1, way],
+            device_id=(slab, lax.rem(group + (1, CASES - 1)[way], CASES)),
+            device_id_type=MESH,
+        )
+        copy.start()
+        sent.append(copy)
+    for dx in (1, 3):
         there = lax.rem(group + dx, CASES)
         copy = pltpu.make_async_remote_copy(
             src_ref=ext.at[pl.ds(there * share, share + 1)],
@@ -303,6 +318,20 @@
 
     field_copy = pltpu.make_async_copy(fields, fields_any, field_sem)
     field_copy.start()
+    for way, (start, many) in enumerate(spans):
+        sent[way].wait_recv()
+        source = lax.rem(group + (CASES - 1, 1)[way], CASES)
+        copy = pltpu.make_async_remote_copy(
+            src_ref=relay.at[way, pl.ds(0, many)],
+            dst_ref=pieces.at[source, pl.ds(start, many)],
+            send_sem=relay_sems.at[2, way],
+            recv_sem=relay_sems.at[3, way],
+            device_id=(slab, lax.rem(group + (1, CASES - 1)[way], CASES)),
+            device_id_type=MESH,
+        )
+        copy.start()
+        sent.append(copy)
+        passed.append(copy)
     every = [
         [pressure[8 * h : 8 * h + 8, 128 * k : 128 * k + 128] for k in range(pressure.shape[1] // 128)]
         for h in range(pressure.shape[0] // 8)
@@ -315,7 +344,9 @@
         loads[pl.ds(j, 1)] = lookup(every, panel[pl.ds(p, 1)]) * factor
 
     keep.wait()
-    for dx in (1, 2, 3):
+    for copy in passed:
+        copy.wait_recv()
+    for dx in (1, 3):
         source = lax.rem(group + dx, CASES)
         pltpu.make_async_remote_copy(
             src_ref=pieces.at[source],
@@ -456,6 +487,8 @@
             pltpu.VMEM((1 + CORES, CASES, cases, width), jnp.float32),
             pltpu.VMEM((ZSIZE, cases, width), jnp.float32),
             pltpu.VMEM((YSIZE, cases, width), jnp.float32),
+            pltpu.VMEM((2, share + 1 - (share + 1) // 2, radial, halves, 8, around), jnp.float32),
+            pltpu.SemaphoreType.DMA((4, 2)),
             pltpu.SemaphoreType.DMA((CASES,)),
             pltpu.SemaphoreType.DMA((CASES,)),
             pltpu.SemaphoreType.DMA((CASES, CORES)),

time: 58.7 us -> 59.5 us (1.014); the launches traced: 58.5 us -> 58.6 us
  no operation moved by 1% of the time
where the time goes in v4:
time: 59.5 us; the launch traced here: 58.6 us
  Pallas kernels  54.9 us (92%)
  local copies, waits for them, and re-layouts  1.77 us (3%)
  other arithmetic  1.32 us (2%)
  between operations  0.65 us (1%)
    pallas_call x1, Pallas kernels, solve(): pl.pallas_call(functools.partial(step_kernel, total), out_shape=[jax.Shap...  36.3 us
    pallas_call x1, Pallas kernels, exchange_halo(): pl.pallas_call(functools.partial(halo_kernel, slabs), out_shape=[jax.Shap...  18.6 us
    unnamed x1, local copies, waits for them, and re-layouts  1.77 us
    mul x1, other arithmetic, local(): return (fields, gram * scale, cross * scale)  1.32 us

profile of v4, /device:TPU:1, one launch (start us, length us, event | category | flops | bytes accessed | tf_op | source)
XLA Modules:
  0.0 58.6 jit_solution(7097808809540178538)
XLA Ops:
  0.6 18.6 %halo.1 = (s32[7,12,4,128]{3,2,1,0:T(4,128)}, s32[7,12,4,128]{3,2,1,0:T(4,128)}, f32[7,12,4,128]{3,2,1,0:T(4,128)}) custom-call(s32[12,4,128]{2,1,0:T(4,128)} %panel.1, s32[12,4,128]{2,1,0:T(4,128)} %flags.1, f32[12,4,128]{2,1,0:T(4,128)} %diagonal.1), custom_call_target="tpu_custom_call" | custom-call | tf_op jit(solution)/shard_map/halo/pallas_call | solution.py:62
  19.2 36.3 %step.1 = (f32[16,12,4,128]{3,2,1,0:T(4,128)}, f32[16,64]{1,0:T(8,128)}, f32[16,64]{1,0:T(8,128)}) custom-call(f32[64,512]{1,0:T(8,128)} %pressure_any.1, s32[84,4,128]{2,1,0:T(4,128)} %bitcast.3, s32[84,4,128]{2,1,0:T(4,128)} %bitcast.4, f32[84,4,128]{2,1,0:T(4,128)} %bitcast.5), custom_call_target="tpu_custom_call" | custom-call | tf_op jit(solution)/shard_map/step/pallas_call | solution.py:472
  55.5 1.3 %broadcast_multiply_fusion = (f32[16,64]{1,0:T(8,128)}, f32[16,64]{1,0:T(8,128)}) fusion(f32[16,64]{1,0:T(8,128)} %get-tuple-element.14, f32[16,64]{1,0:T(8,128)} %get-tuple-element.13), kind=kLoop, calls=%fused_computation | loop fusion | flops 2048 | bytes 16384 | tf_op jit(solution)/shard_map/mul | solution.py:528
  56.8 1.8 %copy.8 = f32[16,12,4,128]{3,2,1,0:T(4,128)} copy(f32[16,12,4,128]{3,2,1,0:T(4,128)} %get-tuple-element.20) | data formatting | bytes 786432

commit v5 on v3

--- a/solution.py
+++ b/solution.py
@@ -379,14 +379,14 @@
             device_id=(slab, group),
             device_id_type=MESH,
         ).wait_recv()
-    total = rows[1, 0]
+    total_rows = rows[1, 0]
     for c in range(CORES):
         for g in range(CASES):
             if (c, g) != (0, 0):
-                total = total + rows[1 + c, g]
-
-    def combine(total, slots, at, size, device, send, recv):
-        slots[at] = total
+                total_rows = total_rows + rows[1 + c, g]
+
+    def spread_out(value, slots, at, size, device, send, recv):
+        slots[at] = value
         for d in range(1, size):
             copy = pltpu.make_async_remote_copy(
                 src_ref=slots.at[at],
@@ -398,6 +398,8 @@
             )
             copy.start()
             sent.append(copy)
+
+    def add_up(slots, at, size, device, send, recv):
         for d in range(1, size):
             source = lax.rem(at + d, size)
             pltpu.make_async_remote_copy(
@@ -413,10 +415,21 @@
             result = result + slots[d]
         return result
 
-    total = combine(total, along_z, z, ZSIZE, z_mate, z_send, z_recv)
-    total = combine(total, along_y, y, YSIZE, y_mate, y_send, y_recv)
-    gram[...] = total[:, :count]
-    cross[...] = total[:, count:]
+    half = total_rows.shape[0] // 2
+    z_way = [(along_z.at[n], z, ZSIZE, z_mate, z_send.at[n], z_recv.at[n]) for n in range(2)]
+    y_way = [(along_y.at[n], y, YSIZE, y_mate, y_send.at[n], y_recv.at[n]) for n in range(2)]
+    spread_out(total_rows[:half], *z_way[0])
+    spread_out(total_rows[half:], *y_way[1])
+    upper = add_up(*z_way[0])
+    spread_out(upper, *y_way[0])
+    lower = add_up(*y_way[1])
+    spread_out(lower, *z_way[1])
+    upper = add_up(*y_way[0])
+    lower = add_up(*z_way[1])
+    gram[:half] = upper[:, :count]
+    gram[half:] = lower[:, :count]
+    cross[:half] = upper[:, count:]
+    cross[half:] = lower[:, count:]
     for copy in sent:
         copy.wait_send()
     field_copy.wait()
@@ -454,16 +467,16 @@
             wide(share),
             pltpu.VMEM((CASES, share + 1, radial, halves, 8, around), jnp.float32),
             pltpu.VMEM((1 + CORES, CASES, cases, width), jnp.float32),
-            pltpu.VMEM((ZSIZE, cases, width), jnp.float32),
-            pltpu.VMEM((YSIZE, cases, width), jnp.float32),
+            pltpu.VMEM((2, ZSIZE, cases // 2, width), jnp.float32),
+            pltpu.VMEM((2, YSIZE, cases // 2, width), jnp.float32),
             pltpu.SemaphoreType.DMA((CASES,)),
             pltpu.SemaphoreType.DMA((CASES,)),
             pltpu.SemaphoreType.DMA((CASES, CORES)),
             pltpu.SemaphoreType.DMA((CORES, CASES)),
-            pltpu.SemaphoreType.DMA((ZSIZE,)),
-            pltpu.SemaphoreType.DMA((ZSIZE,)),
-            pltpu.SemaphoreType.DMA((YSIZE,)),
-            pltpu.SemaphoreType.DMA((YSIZE,)),
+            pltpu.SemaphoreType.DMA((2, ZSIZE)),
+            pltpu.SemaphoreType.DMA((2, ZSIZE)),
+            pltpu.SemaphoreType.DMA((2, YSIZE)),
+            pltpu.SemaphoreType.DMA((2, YSIZE)),
             pltpu.SemaphoreType.DMA,
             field(own + 1),
             pltpu.VMEM(pressure.shape, jnp.float32),

time: 58.7 us -> 58.7 us (level)
  no operation moved by 1% of the time
where the time goes in v5:
time: 58.7 us; the launch traced here: 58.5 us
  Pallas kernels  54.7 us (93%)
  local copies, waits for them, and re-layouts  1.77 us (3%)
  other arithmetic  1.32 us (2%)
  between operations  0.65 us (1%)
    pallas_call x1, Pallas kernels, solve(): pl.pallas_call(functools.partial(step_kernel, total), out_shape=[jax.Shap...  36.1 us
    pallas_call x1, Pallas kernels, exchange_halo(): pl.pallas_call(functools.partial(halo_kernel, slabs), out_shape=[jax.Shap...  18.6 us
    unnamed x1, local copies, waits for them, and re-layouts  1.77 us
    mul x1, other arithmetic, local(): return (fields, gram * scale, cross * scale)  1.32 us

profile of v5, /device:TPU:1, one launch (start us, length us, event | category | flops | bytes accessed | tf_op | source)
XLA Modules:
  0.0 58.5 jit_solution(5063839250401414594)
XLA Ops:
  0.6 18.6 %halo.1 = (s32[7,12,4,128]{3,2,1,0:T(4,128)}, s32[7,12,4,128]{3,2,1,0:T(4,128)}, f32[7,12,4,128]{3,2,1,0:T(4,128)}) custom-call(s32[12,4,128]{2,1,0:T(4,128)} %panel.1, s32[12,4,128]{2,1,0:T(4,128)} %flags.1, f32[12,4,128]{2,1,0:T(4,128)} %diagonal.1), custom_call_target="tpu_custom_call" | custom-call | tf_op jit(solution)/shard_map/halo/pallas_call | solution.py:62
  19.2 36.1 %step.1 = (f32[16,12,4,128]{3,2,1,0:T(4,128)}, f32[16,64]{1,0:T(8,128)}, f32[16,64]{1,0:T(8,128)}) custom-call(f32[64,512]{1,0:T(8,128)} %pressure_any.1, s32[84,4,128]{2,1,0:T(4,128)} %bitcast.3, s32[84,4,128]{2,1,0:T(4,128)} %bitcast.4, f32[84,4,128]{2,1,0:T(4,128)} %bitcast.5), custom_call_target="tpu_custom_call" | custom-call | tf_op jit(solution)/shard_map/step/pallas_call | solution.py:454
  55.4 1.3 %broadcast_multiply_fusion = (f32[16,64]{1,0:T(8,128)}, f32[16,64]{1,0:T(8,128)}) fusion(f32[16,64]{1,0:T(8,128)} %get-tuple-element.14, f32[16,64]{1,0:T(8,128)} %get-tuple-element.13), kind=kLoop, calls=%fused_computation | loop fusion | flops 2048 | bytes 16384 | tf_op jit(solution)/shard_map/mul | solution.py:508
  56.7 1.8 %copy.8 = f32[16,12,4,128]{3,2,1,0:T(4,128)} copy(f32[16,12,4,128]{3,2,1,0:T(4,128)} %get-tuple-element.20) | data formatting | bytes 786432

commit v6 on v5

--- a/solution.py
+++ b/solution.py
@@ -16,7 +16,7 @@
 BASE = 29
 SETUP_STEP = 18
 SWEEP_STEP = 36
-COARSE_STEP = 11
+COARSE_STEP = 33
 highest = lax.Precision.HIGHEST
 
 

time: 58.7 us -> 58.6 us (level)
  no operation moved by 1% of the time
where the time goes in v6:
time: 58.6 us; the launch traced here: 58.3 us
  Pallas kernels  54.6 us (93%)
  local copies, waits for them, and re-layouts  1.77 us (3%)
  other arithmetic  1.32 us (2%)
  between operations  0.65 us (1%)
    pallas_call x1, Pallas kernels, solve(): pl.pallas_call(functools.partial(step_kernel, total), out_shape=[jax.Shap...  36 us
    pallas_call x1, Pallas kernels, exchange_halo(): pl.pallas_call(functools.partial(halo_kernel, slabs), out_shape=[jax.Shap...  18.6 us
    unnamed x1, local copies, waits for them, and re-layouts  1.77 us
    mul x1, other arithmetic, local(): return (fields, gram * scale, cross * scale)  1.32 us

profile of v6, /device:TPU:1, one launch (start us, length us, event | category | flops | bytes accessed | tf_op | source)
XLA Modules:
  0.0 58.3 jit_solution(3715158679083331402)
XLA Ops:
  0.6 18.6 %halo.1 = (s32[7,12,4,128]{3,2,1,0:T(4,128)}, s32[7,12,4,128]{3,2,1,0:T(4,128)}, f32[7,12,4,128]{3,2,1,0:T(4,128)}) custom-call(s32[12,4,128]{2,1,0:T(4,128)} %panel.1, s32[12,4,128]{2,1,0:T(4,128)} %flags.1, f32[12,4,128]{2,1,0:T(4,128)} %diagonal.1), custom_call_target="tpu_custom_call" | custom-call | tf_op jit(solution)/shard_map/halo/pallas_call | solution.py:62
  19.2 36.0 %step.1 = (f32[16,12,4,128]{3,2,1,0:T(4,128)}, f32[16,64]{1,0:T(8,128)}, f32[16,64]{1,0:T(8,128)}) custom-call(f32[64,512]{1,0:T(8,128)} %pressure_any.1, s32[84,4,128]{2,1,0:T(4,128)} %bitcast.3, s32[84,4,128]{2,1,0:T(4,128)} %bitcast.4, f32[84,4,128]{2,1,0:T(4,128)} %bitcast.5), custom_call_target="tpu_custom_call" | custom-call | tf_op jit(solution)/shard_map/step/pallas_call | solution.py:454
  55.2 1.3 %broadcast_multiply_fusion = (f32[16,64]{1,0:T(8,128)}, f32[16,64]{1,0:T(8,128)}) fusion(f32[16,64]{1,0:T(8,128)} %get-tuple-element.14, f32[16,64]{1,0:T(8,128)} %get-tuple-element.13), kind=kLoop, calls=%fused_computation | loop fusion | flops 2048 | bytes 16384 | tf_op jit(solution)/shard_map/mul | solution.py:508
  56.5 1.8 %copy.8 = f32[16,12,4,128]{3,2,1,0:T(4,128)} copy(f32[16,12,4,128]{3,2,1,0:T(4,128)} %get-tuple-element.20) | data formatting | bytes 786432
